TPU v7x, 128 devices: a whole 4x4x4 slice. The times are simulated.
128 devices in a mesh: row: 8 (over z, core), col: 16 (over x, y).
Axes of the slice: x: 4, y: 4, z: 4, core: 2. Of those that a mesh axis runs over, the one named last changes fastest.
Arguments:
- colloc_points: float32 [3, 61440], P(None, 'row'), may hold values from -1 to 1, as said below
- sources: float32 [4, 2048], P(None, 'col'), may hold values from -1 to 1, as said below
- counts: int32 [480, 16], P('row', 'col'), may hold values from 2 to 16, as said below
- row_element: int32 [61440], P('row'), may hold values from 0 to 61439, as said below
- pivots: int32 [128], replicated, may hold values from 0 to 61439, as said below
Outputs:
- factored: float32 [61440, 2048], P('row', 'col')
- u_rows: float32 [128, 2048], P(None, 'col')
Inputs may be any that keep to these rules, and one draw needn't show every extreme that they name: `counts`: every tile uses 2 to 16 quadrature points, and some tile uses 16. `row_element`: a permutation of the 61440 elements. pivots[k] is the row r with row_element[r] == k. `colloc_points`: first two coordinates between 0 and 1, third between -0.1 and 0.1. `sources`: centres as for the collocation points; core radii between 0.05 and 0.15.
All inputs are finite; a program needn't handle non-finite values.
Results may differ from a plain program's by a relative error of at most 0.0003.
Values sent between devices are 32-bit elements; how exact they have to be, the bound alone decides.
No kernel may reach another device: no remote copies, remote signals or barrier semaphores. Data moves between devices by JAX's collectives and lax.ppermute only.
A program may use at most 64 MiB of HBM per device.

v0:
```python
import jax
import jax.numpy as jnp
from jax import lax
from jax.sharding import PartitionSpec as P

QUAD_MAX = 16
jump_factor = 4.0
disc_radius = 4.0
batch_jobs = 32


def from_root(value, axis, root):
    mine = lax.axis_index(axis) == root
    return lax.psum(jnp.where(mine, value, jnp.zeros_like(value)), axis)


def quad_offsets():
    numbers = jnp.arange(QUAD_MAX).astype(jnp.float32)
    radius = disc_radius * jnp.sqrt((numbers + 0.5) / QUAD_MAX)
    angles = 2.39996323 * numbers
    return (radius * jnp.cos(angles), radius * jnp.sin(angles))


def kelvin_entry(point_x, point_y, point_z, source_x, source_y, source_z, source_size):
    delta_x = point_x - source_x
    delta_y = point_y - source_y
    delta_z = point_z - source_z
    rho_sq = delta_x * delta_x + delta_y * delta_y + delta_z * delta_z + source_size * source_size
    return (2.0 + delta_z * delta_z / rho_sq) * lax.rsqrt(rho_sq)


def lower_unit_inverse(lower_unit):
    side = lower_unit.shape[0]
    positions = jnp.arange(side)
    strict = jnp.tril(lower_unit, -1)

    def lower_step(index, inverse):
        unit_row = (positions == index).astype(inverse.dtype)
        strict_row = lax.dynamic_index_in_dim(strict, index, 0, keepdims=False)
        new_row = unit_row - jnp.dot(strict_row, inverse, precision=lax.Precision.HIGHEST)
        return lax.dynamic_update_index_in_dim(inverse, new_row, index, 0)

    return lax.fori_loop(0, side, lower_step, jnp.zeros_like(lower_unit))


def upper_inverse(upper_part):
    side = upper_part.shape[0]
    positions = jnp.arange(side)
    strict = jnp.triu(upper_part, 1)

    def upper_step(count, inverse):
        index = side - 1 - count
        unit_row = (positions == index).astype(inverse.dtype)
        strict_row = lax.dynamic_index_in_dim(strict, index, 0, keepdims=False)
        full_row = lax.dynamic_index_in_dim(upper_part, index, 0, keepdims=False)
        pivot_value = lax.dynamic_index_in_dim(full_row, index, 0, keepdims=False)
        new_row = (
            unit_row - jnp.dot(strict_row, inverse, precision=lax.Precision.HIGHEST)
        ) / pivot_value
        return lax.dynamic_update_index_in_dim(inverse, new_row, index, 0)

    return lax.fori_loop(0, side, upper_step, jnp.zeros_like(upper_part))


def factor_square(square):
    side = square.shape[0]
    positions = jnp.arange(side)

    def eliminate(column, packed):
        pivot_row = lax.dynamic_index_in_dim(packed, column, 0, keepdims=False)
        pivot_col = lax.dynamic_index_in_dim(packed, column, 1, keepdims=False)
        pivot_value = lax.dynamic_index_in_dim(pivot_row, column, 0, keepdims=False)
        under_mask = positions > column
        factor = jnp.where(under_mask, pivot_col / pivot_value, 0.0)
        right_row = jnp.where(under_mask, pivot_row, 0.0)
        packed = packed - factor[:, None] * right_row[None, :]
        return jnp.where(
            (positions[None, :] == column) & under_mask[:, None], factor[:, None], packed
        )

    return lax.fori_loop(0, side, eliminate, square)


def factor_panel(square):
    panel_size = square.shape[0]
    block_width = min(16, panel_size)
    identity = jnp.eye(block_width, dtype=square.dtype)
    packed = square
    for first_col in range(0, panel_size, block_width):
        last_col = first_col + block_width
        diagonal = factor_square(packed[first_col:last_col, first_col:last_col])
        packed = packed.at[first_col:last_col, first_col:last_col].set(diagonal)
        if last_col < panel_size:
            lower_unit = jnp.tril(diagonal, -1) + identity
            upper_part = jnp.triu(diagonal)
            upper_inv = upper_inverse(upper_part)
            lower_inv = lower_unit_inverse(lower_unit)
            left_part = jnp.dot(
                packed[last_col:, first_col:last_col], upper_inv, precision=lax.Precision.HIGHEST
            )
            top_part = jnp.dot(
                lower_inv, packed[first_col:last_col, last_col:], precision=lax.Precision.HIGHEST
            )
            packed = packed.at[last_col:, first_col:last_col].set(left_part)
            packed = packed.at[first_col:last_col, last_col:].set(top_part)
            packed = packed.at[last_col:, last_col:].add(
                -jnp.dot(left_part, top_part, precision=lax.Precision.HIGHEST)
            )
    return packed


def triangle_inverses(square):
    identity = jnp.eye(square.shape[0], dtype=square.dtype)
    packed = factor_panel(square)
    lower_unit = jnp.tril(packed, -1) + identity
    upper_part = jnp.triu(packed)
    return (upper_inverse(upper_part), lower_unit_inverse(lower_unit))


def tile_jobs(buffer, point_tiles, source_tiles, tile_counts, first_job, last_job):
    col_tiles = source_tiles.shape[1]
    offset_x, offset_y = quad_offsets()
    job_ends = jnp.cumsum(tile_counts)
    job_starts = job_ends - tile_counts
    turns = (last_job - first_job + batch_jobs - 1) // batch_jobs

    def one_turn(turn_index, running):
        job_ids = first_job + turn_index * batch_jobs + jnp.arange(batch_jobs)
        live_jobs = job_ids < last_job
        tile_ids = jnp.sum((job_ends[None, :] <= job_ids[:, None]).astype(jnp.int32), axis=1)
        tile_ids = jnp.minimum(tile_ids, tile_counts.shape[0] - 1)
        quad_ids = jnp.clip(job_ids - job_starts[tile_ids], 0, QUAD_MAX - 1)
        row_ids = tile_ids // col_tiles
        col_ids = tile_ids % col_tiles
        points = point_tiles[:, row_ids]
        source = source_tiles[:, col_ids]
        source_size = source[3]
        kernel_values = kelvin_entry(
            points[0][:, :, None],
            points[1][:, :, None],
            points[2][:, :, None],
            (source[0] + source_size * offset_x[quad_ids][:, None])[:, None, :],
            (source[1] + source_size * offset_y[quad_ids][:, None])[:, None, :],
            source[2][:, None, :],
            source_size[:, None, :],
        )
        weight = jnp.where(live_jobs, 1.0 / tile_counts[tile_ids].astype(jnp.float32), 0.0)
        return running.at[tile_ids].add(weight[:, None, None] * kernel_values)

    return lax.fori_loop(0, turns, one_turn, buffer)


def tiles_to_block(buffer, rows_tiles, col_tiles, tile_size):
    shaped = buffer.reshape(rows_tiles, col_tiles, tile_size, tile_size)
    return jnp.transpose(shaped, (0, 2, 1, 3)).reshape(
        rows_tiles * tile_size, col_tiles * tile_size
    )


def pick_rows(source_matrix, pivots, row_offset, local_rows):
    local_ids = pivots - row_offset
    present = (local_ids >= 0) & (local_ids < local_rows)
    picked = source_matrix[jnp.clip(local_ids, 0, local_rows - 1)]
    return jnp.where(present[:, None], picked, 0.0)


def body(colloc_points, sources, counts, row_element, pivots):
    tile_size = pivots.shape[0]
    local_rows = colloc_points.shape[1]
    local_cols = sources.shape[1]
    rows_tiles = local_rows // tile_size
    col_tiles = local_cols // tile_size
    col_index = lax.axis_index("col")
    row_index = lax.axis_index("row")
    row_offset = row_index * local_rows
    jump = jump_factor * tile_size
    point_tiles = colloc_points.reshape(3, rows_tiles, tile_size)
    source_tiles = sources.reshape(4, col_tiles, tile_size)
    own_counts = counts.reshape(-1)
    own_total = jnp.sum(own_counts)
    empty = jnp.zeros((rows_tiles * col_tiles, tile_size, tile_size), jnp.float32)
    assembled_tiles = tile_jobs(empty, point_tiles, source_tiles, own_counts, 0, own_total)
    assembled = tiles_to_block(assembled_tiles, rows_tiles, col_tiles, tile_size)
    column_ids = col_index * local_cols + jnp.arange(local_cols)
    matrix = assembled + jump * (row_element[:, None] == column_ids[None, :]).astype(jnp.float32)
    is_root = col_index == 0
    pivot_rows = lax.psum(pick_rows(matrix, pivots, row_offset, local_rows), "row")
    identity = jnp.eye(tile_size, dtype=jnp.float32)
    square = jnp.where(is_root, pivot_rows, jump * identity)
    upper_inv, lower_inv = triangle_inverses(square)
    root_factor = jnp.dot(
        matrix, upper_inv, precision=lax.Precision.HIGHEST, preferred_element_type=jnp.float32
    )
    panel_factor, lower_inv = (from_root(root_factor, "col", 0), from_root(lower_inv, "col", 0))
    u_rows = jnp.dot(
        lower_inv, pivot_rows, precision=lax.Precision.HIGHEST, preferred_element_type=jnp.float32
    )
    updated = matrix - jnp.dot(
        panel_factor, u_rows, precision=lax.Precision.HIGHEST, preferred_element_type=jnp.float32
    )
    replaced = jnp.concatenate([panel_factor, updated[:, tile_size:]], 1)
    factored = jnp.where(is_root, replaced, updated)
    return (factored, u_rows)


def solution(mesh):
    placed = (P(None, "row"), P(None, "col"), P("row", "col"), P("row"), P())
    return jax.shard_map(
        body,
        mesh=mesh,
        in_specs=placed,
        out_specs=(P("row", "col"), P(None, "col")),
        check_vma=False,
    )
```

profile of v0, /device:TPU:1, one launch (start us, length us, event | category | flops | bytes accessed | tf_op | source)
XLA Modules:
  0.0 1192.0 jit_solution(5250999408835665125)
XLA Ops:
  15.3 108.4 %while.460 = (s32[]{:T(128)}, f32[60,128,128]{2,1,0:T(8,128)}, s32[]{:T(128)}, s32[60]{0:T(128)S(1)}, s32[]{:T(128)}, /*index=5*/s32[60]{0:T(128)S(1)}, f32[3,60...) while((s32[]{:T(128)}, f32[60,128,128]{2,1,0:T(8,128)}, ...), condition=%wide.wide.region_5.6_spmd.clone, body=%wide.wide.region_2.5_spmd.clone.sunk | while | flops 7364899 | bytes 8718849 | solution.py:150
  103.3 6.5 scatter_fusion
  117.0 6.7 scatter_fusion
  123.7 6.9 bitcast_add_fusion
  135.7 323.9 %all-reduce.4.cloned.1.call-done = f32[128,128]{1,0:T(8,128)} async-done(((f32[128,128]{1,0:T(8,128)}), f32[128,128]{1,0:T(8,128)}) %all-reduce.4.cloned.1.call-update) | async-done | bytes 65552 | tf_op jit(solution)/shard_map/psum | solution.py:187
  460.6 22.7 %while.452 = (s32[]{:T(128)}, f32[16,16]{0,1:T(8,128)S(1)}, s32[]{:T(128)}, s32[]{:T(128)}, s32[]{:T(128)}) while((s32[]{:T(128)}, f32[16,16]{0,1:T(8,128)S(1)}, s32[]{:T(128)}, s32[]{:T(128)}, s32[]{:T(128)}) %tuple.1103), condition=%wide.region_8.9_spmd.clone.clone, body=%wide.region_7.8_spmd.clone.clone.sunk | while | flops 1139 | bytes 6697 | solution.py:81
  483.9 22.6 %while.436 = (s32[]{:T(128)}, f32[16,16]{1,0:T(8,128)S(1)}, f32[16,16]{1,0:T(8,128)S(1)}, f32[16,16]{0,1:T(8,128)S(1)}, s32[]{:T(128)}, /*index=5*/s32[]{:T(128)}, s32[]{:T(128)}, s32[]{:T(128)}) while((s32[]{:T(128)}, f32[16,16]{1,0:T(8,128)S(1)}, f32[16,16]{1,0:T(8,128)S(1)}, f32[16,16]{0,1:T(8,128)S(1)}, s32[]{:T(128)}, ...), condition=%wide.region_10.11_spmd.clone, body=%wide.region_9.10_spmd.clone.sunk | while | flops 3143 | bytes 9079 | solution.py:62
  516.6 22.7 %while.453 = (s32[]{:T(128)}, f32[16,16]{0,1:T(8,128)S(1)}, s32[]{:T(128)}, s32[]{:T(128)}, s32[]{:T(128)}) while((s32[]{:T(128)}, f32[16,16]{0,1:T(8,128)S(1)}, s32[]{:T(128)}, s32[]{:T(128)}, s32[]{:T(128)}) %tuple.1112), condition=%wide.region_15.16_spmd.clone.clone, body=%wide.region_14.15_spmd.clone.clone.sunk | while | flops 1139 | bytes 6697 | solution.py:81
  539.5 22.6 %while.438 = (s32[]{:T(128)}, f32[16,16]{1,0:T(8,128)S(1)}, f32[16,16]{1,0:T(8,128)S(1)}, f32[16,16]{0,1:T(8,128)S(1)}, s32[]{:T(128)}, /*index=5*/s32[]{:T(128)}, s32[]{:T(128)}, s32[]{:T(128)}) while((s32[]{:T(128)}, f32[16,16]{1,0:T(8,128)S(1)}, f32[16,16]{1,0:T(8,128)S(1)}, f32[16,16]{0,1:T(8,128)S(1)}, s32[]{:T(128)}, ...), condition=%wide.region_17.18_spmd.clone, body=%wide.region_16.17_spmd.clone.sunk | while | flops 3143 | bytes 9079 | solution.py:62
  569.9 22.7 %while.454 = (s32[]{:T(128)}, f32[16,16]{0,1:T(8,128)S(1)}, s32[]{:T(128)}, s32[]{:T(128)}, s32[]{:T(128)}) while((s32[]{:T(128)}, f32[16,16]{0,1:T(8,128)S(1)}, s32[]{:T(128)}, s32[]{:T(128)}, s32[]{:T(128)}) %tuple.1121), condition=%wide.region_21.22_spmd.clone.clone, body=%wide.region_20.21_spmd.clone.clone.sunk | while | flops 1139 | bytes 6697 | solution.py:81
  592.7 22.6 %while.440 = (s32[]{:T(128)}, f32[16,16]{1,0:T(8,128)S(1)}, f32[16,16]{1,0:T(8,128)S(1)}, f32[16,16]{0,1:T(8,128)S(1)}, s32[]{:T(128)}, /*index=5*/s32[]{:T(128)}, s32[]{:T(128)}, s32[]{:T(128)}) while((s32[]{:T(128)}, f32[16,16]{1,0:T(8,128)S(1)}, f32[16,16]{1,0:T(8,128)S(1)}, f32[16,16]{0,1:T(8,128)S(1)}, s32[]{:T(128)}, ...), condition=%wide.region_23.24_spmd.clone, body=%wide.region_22.23_spmd.clone.sunk | while | flops 3143 | bytes 9079 | solution.py:62
  622.9 22.7 %while.455 = (s32[]{:T(128)}, f32[16,16]{0,1:T(8,128)S(1)}, s32[]{:T(128)}, s32[]{:T(128)}, s32[]{:T(128)}) while((s32[]{:T(128)}, f32[16,16]{0,1:T(8,128)S(1)}, s32[]{:T(128)}, s32[]{:T(128)}, s32[]{:T(128)}) %tuple.1130), condition=%wide.region_27.28_spmd.clone.clone, body=%wide.region_26.27_spmd.clone.clone.sunk | while | flops 1139 | bytes 6697 | solution.py:81
  645.8 22.6 %while.442 = (s32[]{:T(128)}, f32[16,16]{1,0:T(8,128)S(1)}, f32[16,16]{1,0:T(8,128)S(1)}, f32[16,16]{0,1:T(8,128)S(1)}, s32[]{:T(128)}, /*index=5*/s32[]{:T(128)}, s32[]{:T(128)}, s32[]{:T(128)}) while((s32[]{:T(128)}, f32[16,16]{1,0:T(8,128)S(1)}, f32[16,16]{1,0:T(8,128)S(1)}, f32[16,16]{0,1:T(8,128)S(1)}, s32[]{:T(128)}, ...), condition=%wide.region_29.30_spmd.clone, body=%wide.region_28.29_spmd.clone.sunk | while | flops 3143 | bytes 9079 | solution.py:62
  675.7 22.7 %while.456 = (s32[]{:T(128)}, f32[16,16]{0,1:T(8,128)S(1)}, s32[]{:T(128)}, s32[]{:T(128)}, s32[]{:T(128)}) while((s32[]{:T(128)}, f32[16,16]{0,1:T(8,128)S(1)}, s32[]{:T(128)}, s32[]{:T(128)}, s32[]{:T(128)}) %tuple.1139), condition=%wide.region_33.34_spmd.clone.clone, body=%wide.region_32.33_spmd.clone.clone.sunk | while | flops 1139 | bytes 6697 | solution.py:81
  698.5 22.6 %while.444 = (s32[]{:T(128)}, f32[16,16]{1,0:T(8,128)S(1)}, f32[16,16]{1,0:T(8,128)S(1)}, f32[16,16]{0,1:T(8,128)S(1)}, s32[]{:T(128)}, /*index=5*/s32[]{:T(128)}, s32[]{:T(128)}, s32[]{:T(128)}) while((s32[]{:T(128)}, f32[16,16]{1,0:T(8,128)S(1)}, f32[16,16]{1,0:T(8,128)S(1)}, f32[16,16]{0,1:T(8,128)S(1)}, s32[]{:T(128)}, ...), condition=%wide.region_35.36_spmd.clone, body=%wide.region_34.35_spmd.clone.sunk | while | flops 3143 | bytes 9079 | solution.py:62
  728.4 22.7 %while.457 = (s32[]{:T(128)}, f32[16,16]{0,1:T(8,128)S(1)}, s32[]{:T(128)}, s32[]{:T(128)}, s32[]{:T(128)}) while((s32[]{:T(128)}, f32[16,16]{0,1:T(8,128)S(1)}, s32[]{:T(128)}, s32[]{:T(128)}, s32[]{:T(128)}) %tuple.1148), condition=%wide.region_39.40_spmd.clone.clone, body=%wide.region_38.39_spmd.clone.clone.sunk | while | flops 1139 | bytes 6697 | solution.py:81
  751.2 22.6 %while.446 = (s32[]{:T(128)}, f32[16,16]{1,0:T(8,128)S(1)}, f32[16,16]{1,0:T(8,128)S(1)}, f32[16,16]{0,1:T(8,128)S(1)}, s32[]{:T(128)}, /*index=5*/s32[]{:T(128)}, s32[]{:T(128)}, s32[]{:T(128)}) while((s32[]{:T(128)}, f32[16,16]{1,0:T(8,128)S(1)}, f32[16,16]{1,0:T(8,128)S(1)}, f32[16,16]{0,1:T(8,128)S(1)}, s32[]{:T(128)}, ...), condition=%wide.region_41.42_spmd.clone, body=%wide.region_40.41_spmd.clone.sunk | while | flops 3143 | bytes 9079 | solution.py:62
  781.0 22.7 %while.458 = (s32[]{:T(128)}, f32[16,16]{0,1:T(8,128)S(1)}, s32[]{:T(128)}, s32[]{:T(128)}, s32[]{:T(128)}) while((s32[]{:T(128)}, f32[16,16]{0,1:T(8,128)S(1)}, s32[]{:T(128)}, s32[]{:T(128)}, s32[]{:T(128)}) %tuple.1157), condition=%wide.region_45.46_spmd.clone.clone, body=%wide.region_44.45_spmd.clone.clone.sunk | while | flops 1139 | bytes 6697 | solution.py:81
  803.8 22.6 %while.448 = (s32[]{:T(128)}, f32[16,16]{1,0:T(8,128)S(1)}, f32[16,16]{1,0:T(8,128)S(1)}, f32[16,16]{0,1:T(8,128)S(1)}, s32[]{:T(128)}, /*index=5*/s32[]{:T(128)}, s32[]{:T(128)}, s32[]{:T(128)}) while((s32[]{:T(128)}, f32[16,16]{1,0:T(8,128)S(1)}, f32[16,16]{1,0:T(8,128)S(1)}, f32[16,16]{0,1:T(8,128)S(1)}, s32[]{:T(128)}, ...), condition=%wide.region_47.48_spmd.clone, body=%wide.region_46.47_spmd.clone.sunk | while | flops 3143 | bytes 9079 | solution.py:62
  833.0 22.7 %while.459 = (s32[]{:T(128)}, f32[16,16]{0,1:T(8,128)S(1)}, s32[]{:T(128)}, s32[]{:T(128)}, s32[]{:T(128)}) while((s32[]{:T(128)}, f32[16,16]{0,1:T(8,128)S(1)}, s32[]{:T(128)}, s32[]{:T(128)}, s32[]{:T(128)}) %tuple.1166), condition=%wide.region_51.52_spmd.clone.clone, body=%wide.region_50.51_spmd.clone.clone.sunk | while | flops 1139 | bytes 6697 | solution.py:81
  856.5 185.1 %while.450 = (s32[]{:T(128)}, f32[128,128]{1,0:T(8,128)S(1)}, f32[128,128]{1,0:T(8,128)S(1)}, f32[128,128]{1,0:T(8,128)S(1)}, s32[]{:T(128)}, /*index=5*/s32[]{:T(128)}, s32[]{:T(128)}, s32[]{:T(128)}) while((s32[]{:T(128)}, f32[128,128]{1,0:T(8,128)S(1)}, f32[128,128]{1,0:T(8,128)S(1)}, f32[128,128]{1,0:T(8,128)S(1)}, ...), condition=%wide.region_53.54_spmd.clone, body=%wide.region_52.53_spmd.clone.sunk | while | flops 197127 | bytes 67767 | solution.py:62
  1041.7 26.2 %while.451 = (s32[]{:T(128)}, f32[128,128]{1,0:T(8,128)S(1)}, f32[128,128]{1,0:T(8,128)S(1)}, s32[]{:T(128)}, s32[]{:T(128)}) while((s32[]{:T(128)}, f32[128,128]{1,0:T(8,128)S(1)}, f32[128,128]{1,0:T(8,128)S(1)}, s32[]{:T(128)}, s32[]{:T(128)}) %tuple.1172), condition=%wide.region_56.57_spmd.clone, body=%wide.region_55.56_spmd.clone.sunk | while | flops 196994 | bytes 68681 | solution.py:43
  1074.7 101.5 %all-reduce.6.cloned.1.call-done = (f32[7680,128]{1,0:T(8,128)}, f32[128,128]{1,0:T(8,128)}) async-done(((f32[7680,128]{1,0:T(8,128)}, f32[128,128]{1,0:T(8,128)}), (f32[7680,128]{1,0:T(8,128)}, f32[128,128]{1,0:T(8,128)})) %all-reduce.6.cloned.1.call-update) | async-done | bytes 3997712 | tf_op jit(solution)/shard_map/psum | solution.py:14
  1177.3 7.8 fusion.159
  (2281 shorter events, 729.7 us)
Async XLA Ops:
  7.2 8.2 copy-start
  7.2 8.1 copy-start.3
  7.2 452.5 %all-reduce.4.cloned.1.call-start = ((), (), s32[]{:S(2)}) async-start(), calls=%async_computation | async-start | bytes 131072 | tf_op jit(solution)/shard_map/psum | solution.py:187
  15.3 108.4 %copy-start.4 = (s32[7680]{0:T(1024)S(1)}, s32[7680]{0:T(1024)}, u32[]{:S(2)}) copy-start(s32[7680]{0:T(1024)} %param.116) | copy-start | bytes 92164
  123.7 10.7 copy-start.5
  134.1 1042.2 %all-reduce.6.cloned.1.call-start = ((), (), s32[]{:S(2)}) async-start(), calls=%async_computation.1 | async-start | bytes 7995392 | tf_op jit(solution)/shard_map/psum | solution.py:14
  1074.7 101.6 %copy-start.2 = (f32[128,128]{1,0:T(8,128)S(1)}, f32[128,128]{1,0:T(8,128)}, u32[]{:S(2)}) copy-start(f32[128,128]{1,0:T(8,128)} %all-reduce.4.cloned.1.call-done) | copy-start | bytes 196612
  1177.3 7.8 copy-start.1
Sparse Core Ops, SparseCore 0:
  134.2 325.3 all-reduce.3
  1074.9 101.3 all-reduce.5
where the time goes:
time: 1200 us; the launch traced here: 1190 us
  waiting for transfers between devices  426 us (36%)
  local copies, waits for them, and re-layouts  310 us (26%)
  matrix products  245 us (20%)
  other arithmetic  183 us (15%)
  between operations  15.4 us (1%)
  loops' own time  13.1 us (1%)
    psum x1, waiting for transfers between devices, body(): lax.psum(pick_rows(matrix, pivots, row_offset, local_rows), 'row')  324 us
    dot_general x240, matrix products, upper_step(): jnp.dot(strict_row, inverse, precision=lax.Precision.HIGHEST)  189 us
    dynamic_slice x240, local copies, waits for them, and re-layouts, upper_step(): pivot_value = lax.dynamic_index_in_dim(full_row, index, 0, keepdims=False)  141 us
    psum x1, waiting for transfers between devices, from_root(): return lax.psum(jnp.where(mine, value, jnp.zeros_like(value)), axis)  102 us
    broadcast_in_dim x128, other arithmetic, eliminate(): jnp.where((positions[None, :] == column) & under_mask[:, None], factor[:,...  83.7 us
    dynamic_slice x128, local copies, waits for them, and re-layouts, eliminate(): pivot_value = lax.dynamic_index_in_dim(pivot_row, column, 0, keepdims=False)  75 us
    scatter-add x8, other arithmetic, one_turn(): return running.at[tile_ids].add(weight[:, None, None] * kernel_values)  50.6 us
    dot_general x240, matrix products, lower_step(): jnp.dot(strict_row, inverse, precision=lax.Precision.HIGHEST)  34.7 us
  transfers between devices with their start and end apart: 2, of which 2 were waited for; matrix products, arithmetic and copies ran while one was open for 0% of the time, Pallas kernels for 0%

commit v1 on v0

--- a/solution.py
+++ b/solution.py
@@ -184,7 +184,9 @@
     column_ids = col_index * local_cols + jnp.arange(local_cols)
     matrix = assembled + jump * (row_element[:, None] == column_ids[None, :]).astype(jnp.float32)
     is_root = col_index == 0
-    pivot_rows = lax.psum(pick_rows(matrix, pivots, row_offset, local_rows), "row")
+    pivot_rows = jnp.sum(
+        lax.all_gather(pick_rows(matrix, pivots, row_offset, local_rows), "row"), axis=0
+    )
     identity = jnp.eye(tile_size, dtype=jnp.float32)
     square = jnp.where(is_root, pivot_rows, jump * identity)
     upper_inv, lower_inv = triangle_inverses(square)

time: 1200 us -> 1160 us (0.967)
  waiting for transfers between devices: 426 us -> 353 us
  blocking collectives: 0 us -> 29.4 us
    psum x1 -> x0, waiting for transfers between devices: 324 us -> none  [body(): lax.psum(pick_rows(matrix, pivots, row_offset, local_rows), 'row')]
    psum x1, waiting for transfers between devices: 102 us -> 353 us  [from_root(): return lax.psum(jnp.where(mine, value, jnp.zeros_like(value)), axis)]
    all_gather x0 -> x1, blocking collectives: none -> 29.4 us  [body(): lax.all_gather(pick_rows(matrix, pivots, row_offset, local_rows), 'row')]
  transfers between devices with their start and end apart: 2 -> 1, of which waited for: 2 -> 1; matrix products, arithmetic and copies ran while one was open for 0% -> 0% of each run, Pallas kernels for 0% -> 0%
where the time goes in v1:
time: 1160 us; the launch traced here: 1150 us
  waiting for transfers between devices  353 us (30%)
  local copies, waits for them, and re-layouts  310 us (27%)
  matrix products  245 us (21%)
  other arithmetic  182 us (16%)
  blocking collectives  29.4 us (3%)
  between operations  15.4 us (1%)
  loops' own time  13.3 us (1%)
    psum x1, waiting for transfers between devices, from_root(): return lax.psum(jnp.where(mine, value, jnp.zeros_like(value)), axis)  353 us
    dot_general x240, matrix products, upper_step(): jnp.dot(strict_row, inverse, precision=lax.Precision.HIGHEST)  189 us
    dynamic_slice x240, local copies, waits for them, and re-layouts, upper_step(): pivot_value = lax.dynamic_index_in_dim(full_row, index, 0, keepdims=False)  141 us
    broadcast_in_dim x128, other arithmetic, eliminate(): jnp.where((positions[None, :] == column) & under_mask[:, None], factor[:,...  83.7 us
    dynamic_slice x128, local copies, waits for them, and re-layouts, eliminate(): pivot_value = lax.dynamic_index_in_dim(pivot_row, column, 0, keepdims=False)  75 us
    scatter-add x8, other arithmetic, one_turn(): return running.at[tile_ids].add(weight[:, None, None] * kernel_values)  50.6 us
    dot_general x240, matrix products, lower_step(): jnp.dot(strict_row, inverse, precision=lax.Precision.HIGHEST)  34.7 us
    all_gather x1, blocking collectives, body(): lax.all_gather(pick_rows(matrix, pivots, row_offset, local_rows), 'row')  29.4 us
  transfers between devices with their start and end apart: 1, of which 1 were waited for; matrix products, arithmetic and copies ran while one was open for 0% of the time, Pallas kernels for 0%

profile of v1, /device:TPU:1, one launch (start us, length us, event | category | flops | bytes accessed | tf_op | source)
XLA Modules:
  0.0 1148.0 jit_solution(7541935678759782424)
XLA Ops:
  17.3 108.5 %while.460 = (s32[]{:T(128)}, f32[60,128,128]{2,1,0:T(8,128)}, s32[]{:T(128)}, s32[60]{0:T(128)S(1)}, s32[]{:T(128)}, /*index=5*/s32[60]{0:T(128)S(1)}, f32[3,60...) while((s32[]{:T(128)}, f32[60,128,128]{2,1,0:T(8,128)}, ...), condition=%wide.wide.region_5.6_spmd.clone, body=%wide.wide.region_2.5_spmd.clone.sunk | while | flops 7364899 | bytes 8718849 | solution.py:150
  105.5 6.5 scatter_fusion
  119.2 6.7 scatter_fusion
  125.9 6.9 bitcast_add_fusion
  135.6 29.4 %all_gather.4 = f32[8,128,128]{2,1,0:T(8,128)S(1)} all-gather(f32[1,128,128]{2,1,0:T(8,128)S(1)} %bitcast_select_fusion.16), channel_id=1, replica_groups=mesh['row'=8,'col'=16] {'row'}, dimensions={0}, use_global_device_ids=true | all-gather | bytes 589824 | tf_op jit(solution)/shard_map/all_gather | solution.py:188
  165.1 22.8 %while.452 = (s32[]{:T(128)}, f32[16,16]{0,1:T(8,128)S(1)}, s32[]{:T(128)}, s32[]{:T(128)}, s32[]{:T(128)}) while((s32[]{:T(128)}, f32[16,16]{0,1:T(8,128)S(1)}, s32[]{:T(128)}, s32[]{:T(128)}, s32[]{:T(128)}) %tuple.1125), condition=%wide.region_8.9_spmd.clone.clone, body=%wide.region_7.8_spmd.clone.clone.sunk | while | flops 1139 | bytes 6697 | solution.py:81
  188.6 22.6 %while.436 = (s32[]{:T(128)}, f32[16,16]{1,0:T(8,128)S(1)}, f32[16,16]{1,0:T(8,128)S(1)}, f32[16,16]{0,1:T(8,128)S(1)}, s32[]{:T(128)}, /*index=5*/s32[]{:T(128)}, s32[]{:T(128)}, s32[]{:T(128)}) while((s32[]{:T(128)}, f32[16,16]{1,0:T(8,128)S(1)}, f32[16,16]{1,0:T(8,128)S(1)}, f32[16,16]{0,1:T(8,128)S(1)}, s32[]{:T(128)}, ...), condition=%wide.region_10.11_spmd.clone, body=%wide.region_9.10_spmd.clone.sunk | while | flops 3143 | bytes 9079 | solution.py:62
  221.2 22.7 %while.453 = (s32[]{:T(128)}, f32[16,16]{0,1:T(8,128)S(1)}, s32[]{:T(128)}, s32[]{:T(128)}, s32[]{:T(128)}) while((s32[]{:T(128)}, f32[16,16]{0,1:T(8,128)S(1)}, s32[]{:T(128)}, s32[]{:T(128)}, s32[]{:T(128)}) %tuple.1134), condition=%wide.region_15.16_spmd.clone.clone, body=%wide.region_14.15_spmd.clone.clone.sunk | while | flops 1139 | bytes 6697 | solution.py:81
  244.0 22.6 %while.438 = (s32[]{:T(128)}, f32[16,16]{1,0:T(8,128)S(1)}, f32[16,16]{1,0:T(8,128)S(1)}, f32[16,16]{0,1:T(8,128)S(1)}, s32[]{:T(128)}, /*index=5*/s32[]{:T(128)}, s32[]{:T(128)}, s32[]{:T(128)}) while((s32[]{:T(128)}, f32[16,16]{1,0:T(8,128)S(1)}, f32[16,16]{1,0:T(8,128)S(1)}, f32[16,16]{0,1:T(8,128)S(1)}, s32[]{:T(128)}, ...), condition=%wide.region_17.18_spmd.clone, body=%wide.region_16.17_spmd.clone.sunk | while | flops 3143 | bytes 9079 | solution.py:62
  274.4 22.7 %while.454 = (s32[]{:T(128)}, f32[16,16]{0,1:T(8,128)S(1)}, s32[]{:T(128)}, s32[]{:T(128)}, s32[]{:T(128)}) while((s32[]{:T(128)}, f32[16,16]{0,1:T(8,128)S(1)}, s32[]{:T(128)}, s32[]{:T(128)}, s32[]{:T(128)}) %tuple.1143), condition=%wide.region_21.22_spmd.clone.clone, body=%wide.region_20.21_spmd.clone.clone.sunk | while | flops 1139 | bytes 6697 | solution.py:81
  297.2 22.6 %while.440 = (s32[]{:T(128)}, f32[16,16]{1,0:T(8,128)S(1)}, f32[16,16]{1,0:T(8,128)S(1)}, f32[16,16]{0,1:T(8,128)S(1)}, s32[]{:T(128)}, /*index=5*/s32[]{:T(128)}, s32[]{:T(128)}, s32[]{:T(128)}) while((s32[]{:T(128)}, f32[16,16]{1,0:T(8,128)S(1)}, f32[16,16]{1,0:T(8,128)S(1)}, f32[16,16]{0,1:T(8,128)S(1)}, s32[]{:T(128)}, ...), condition=%wide.region_23.24_spmd.clone, body=%wide.region_22.23_spmd.clone.sunk | while | flops 3143 | bytes 9079 | solution.py:62
  327.4 22.7 %while.455 = (s32[]{:T(128)}, f32[16,16]{0,1:T(8,128)S(1)}, s32[]{:T(128)}, s32[]{:T(128)}, s32[]{:T(128)}) while((s32[]{:T(128)}, f32[16,16]{0,1:T(8,128)S(1)}, s32[]{:T(128)}, s32[]{:T(128)}, s32[]{:T(128)}) %tuple.1152), condition=%wide.region_27.28_spmd.clone.clone, body=%wide.region_26.27_spmd.clone.clone.sunk | while | flops 1139 | bytes 6697 | solution.py:81
  350.3 22.6 %while.442 = (s32[]{:T(128)}, f32[16,16]{1,0:T(8,128)S(1)}, f32[16,16]{1,0:T(8,128)S(1)}, f32[16,16]{0,1:T(8,128)S(1)}, s32[]{:T(128)}, /*index=5*/s32[]{:T(128)}, s32[]{:T(128)}, s32[]{:T(128)}) while((s32[]{:T(128)}, f32[16,16]{1,0:T(8,128)S(1)}, f32[16,16]{1,0:T(8,128)S(1)}, f32[16,16]{0,1:T(8,128)S(1)}, s32[]{:T(128)}, ...), condition=%wide.region_29.30_spmd.clone, body=%wide.region_28.29_spmd.clone.sunk | while | flops 3143 | bytes 9079 | solution.py:62
  380.2 22.7 %while.456 = (s32[]{:T(128)}, f32[16,16]{0,1:T(8,128)S(1)}, s32[]{:T(128)}, s32[]{:T(128)}, s32[]{:T(128)}) while((s32[]{:T(128)}, f32[16,16]{0,1:T(8,128)S(1)}, s32[]{:T(128)}, s32[]{:T(128)}, s32[]{:T(128)}) %tuple.1161), condition=%wide.region_33.34_spmd.clone.clone, body=%wide.region_32.33_spmd.clone.clone.sunk | while | flops 1139 | bytes 6697 | solution.py:81
  403.0 22.6 %while.444 = (s32[]{:T(128)}, f32[16,16]{1,0:T(8,128)S(1)}, f32[16,16]{1,0:T(8,128)S(1)}, f32[16,16]{0,1:T(8,128)S(1)}, s32[]{:T(128)}, /*index=5*/s32[]{:T(128)}, s32[]{:T(128)}, s32[]{:T(128)}) while((s32[]{:T(128)}, f32[16,16]{1,0:T(8,128)S(1)}, f32[16,16]{1,0:T(8,128)S(1)}, f32[16,16]{0,1:T(8,128)S(1)}, s32[]{:T(128)}, ...), condition=%wide.region_35.36_spmd.clone, body=%wide.region_34.35_spmd.clone.sunk | while | flops 3143 | bytes 9079 | solution.py:62
  432.9 22.7 %while.457 = (s32[]{:T(128)}, f32[16,16]{0,1:T(8,128)S(1)}, s32[]{:T(128)}, s32[]{:T(128)}, s32[]{:T(128)}) while((s32[]{:T(128)}, f32[16,16]{0,1:T(8,128)S(1)}, s32[]{:T(128)}, s32[]{:T(128)}, s32[]{:T(128)}) %tuple.1170), condition=%wide.region_39.40_spmd.clone.clone, body=%wide.region_38.39_spmd.clone.clone.sunk | while | flops 1139 | bytes 6697 | solution.py:81
  455.7 22.6 %while.446 = (s32[]{:T(128)}, f32[16,16]{1,0:T(8,128)S(1)}, f32[16,16]{1,0:T(8,128)S(1)}, f32[16,16]{0,1:T(8,128)S(1)}, s32[]{:T(128)}, /*index=5*/s32[]{:T(128)}, s32[]{:T(128)}, s32[]{:T(128)}) while((s32[]{:T(128)}, f32[16,16]{1,0:T(8,128)S(1)}, f32[16,16]{1,0:T(8,128)S(1)}, f32[16,16]{0,1:T(8,128)S(1)}, s32[]{:T(128)}, ...), condition=%wide.region_41.42_spmd.clone, body=%wide.region_40.41_spmd.clone.sunk | while | flops 3143 | bytes 9079 | solution.py:62
  485.5 22.7 %while.458 = (s32[]{:T(128)}, f32[16,16]{0,1:T(8,128)S(1)}, s32[]{:T(128)}, s32[]{:T(128)}, s32[]{:T(128)}) while((s32[]{:T(128)}, f32[16,16]{0,1:T(8,128)S(1)}, s32[]{:T(128)}, s32[]{:T(128)}, s32[]{:T(128)}) %tuple.1179), condition=%wide.region_45.46_spmd.clone.clone, body=%wide.region_44.45_spmd.clone.clone.sunk | while | flops 1139 | bytes 6697 | solution.py:81
  508.4 22.6 %while.448 = (s32[]{:T(128)}, f32[16,16]{1,0:T(8,128)S(1)}, f32[16,16]{1,0:T(8,128)S(1)}, f32[16,16]{0,1:T(8,128)S(1)}, s32[]{:T(128)}, /*index=5*/s32[]{:T(128)}, s32[]{:T(128)}, s32[]{:T(128)}) while((s32[]{:T(128)}, f32[16,16]{1,0:T(8,128)S(1)}, f32[16,16]{1,0:T(8,128)S(1)}, f32[16,16]{0,1:T(8,128)S(1)}, s32[]{:T(128)}, ...), condition=%wide.region_47.48_spmd.clone, body=%wide.region_46.47_spmd.clone.sunk | while | flops 3143 | bytes 9079 | solution.py:62
  537.5 22.7 %while.459 = (s32[]{:T(128)}, f32[16,16]{0,1:T(8,128)S(1)}, s32[]{:T(128)}, s32[]{:T(128)}, s32[]{:T(128)}) while((s32[]{:T(128)}, f32[16,16]{0,1:T(8,128)S(1)}, s32[]{:T(128)}, s32[]{:T(128)}, s32[]{:T(128)}) %tuple.1188), condition=%wide.region_51.52_spmd.clone.clone, body=%wide.region_50.51_spmd.clone.clone.sunk | while | flops 1139 | bytes 6697 | solution.py:81
  561.0 185.1 %while.450 = (s32[]{:T(128)}, f32[128,128]{1,0:T(8,128)S(1)}, f32[128,128]{1,0:T(8,128)S(1)}, f32[128,128]{1,0:T(8,128)S(1)}, s32[]{:T(128)}, /*index=5*/s32[]{:T(128)}, s32[]{:T(128)}, s32[]{:T(128)}) while((s32[]{:T(128)}, f32[128,128]{1,0:T(8,128)S(1)}, f32[128,128]{1,0:T(8,128)S(1)}, f32[128,128]{1,0:T(8,128)S(1)}, ...), condition=%wide.region_53.54_spmd.clone, body=%wide.region_52.53_spmd.clone.sunk | while | flops 197127 | bytes 67767 | solution.py:62
  746.2 26.2 %while.451 = (s32[]{:T(128)}, f32[128,128]{1,0:T(8,128)S(1)}, f32[128,128]{1,0:T(8,128)S(1)}, s32[]{:T(128)}, s32[]{:T(128)}) while((s32[]{:T(128)}, f32[128,128]{1,0:T(8,128)S(1)}, f32[128,128]{1,0:T(8,128)S(1)}, s32[]{:T(128)}, s32[]{:T(128)}) %tuple.1194), condition=%wide.region_56.57_spmd.clone, body=%wide.region_55.56_spmd.clone.sunk | while | flops 196994 | bytes 68681 | solution.py:43
  779.3 353.0 %all-reduce.3.cloned.1.call-done = (f32[7680,128]{1,0:T(8,128)}, f32[128,128]{1,0:T(8,128)}) async-done(((f32[7680,128]{1,0:T(8,128)}, f32[128,128]{1,0:T(8,128)}), (f32[7680,128]{1,0:T(8,128)}, f32[128,128]{1,0:T(8,128)})) %all-reduce.3.cloned.1.call-update) | async-done | bytes 3997712 | tf_op jit(solution)/shard_map/psum | solution.py:14
  1133.3 7.9 fusion.159
  (2276 shorter events, 728.6 us)
Async XLA Ops:
  7.2 10.2 copy-start
  7.2 10.2 copy-start.2
  7.2 1125.0 %all-reduce.3.cloned.1.call-start = ((), (), s32[]{:S(2)}) async-start(), calls=%async_computation | async-start | bytes 7995392 | tf_op jit(solution)/shard_map/psum | solution.py:14
  17.3 108.5 %copy-start.3 = (s32[7680]{0:T(1024)S(1)}, s32[7680]{0:T(1024)}, u32[]{:S(2)}) copy-start(s32[7680]{0:T(1024)} %param.116) | copy-start | bytes 92164
  1133.3 7.9 copy-start.1
Sparse Core Ops, SparseCore 0:
  779.4 352.7 all-reduce.2
